TPU v7x, 256 devices: a whole 4x4x8 slice. The times are simulated.
256 devices in a mesh: leaf: 64 (over y, z, core), front: 4 (over x).
Axes of the slice: x: 4, y: 4, z: 8, core: 2. Of those that a mesh axis runs over, the one named last changes fastest.
Arguments:
- rhs_sub: float32 [8, 524288], P(None, ('leaf', 'front')), may hold values from -6 to 6
- rhs_sep: float32 [8, 16384], P(None, 'leaf'), may hold values from -6 to 6
- live_rows: int32 [256], P(('leaf', 'front')), may hold values from 256 to 2048, as said below
- lower_inv: bfloat16 [2048, 256, 256], P(('leaf', 'front')), as said below
- upper_inv: bfloat16 [2048, 256, 256], P(('leaf', 'front'))
- couple_low: bfloat16 [16384, 16384], P(('leaf', 'front')), may hold values from -0.1875 to 0.1875
- couple_up: bfloat16 [16384, 16384], P(('leaf', 'front')), may hold values from -0.046875 to 0.046875
- sep_lower_inv: bfloat16 [16384, 16384], P('leaf', 'front')
- sep_upper_inv: bfloat16 [16384, 16384], P('leaf', 'front')
- basis_sub: float32 [48, 524288], P(None, ('leaf', 'front')), may hold values from -0.0078125 to 0.0078125
- basis_sep: float32 [48, 16384], P(None, 'leaf'), may hold values from -0.0078125 to 0.0078125
Outputs:
- orth_sub: float32 [8, 524288], P(None, ('leaf', 'front'))
- orth_sep: float32 [8, 16384], P(None, 'leaf')
- coef: float32 [48, 8], replicated
Inputs may be any that keep to these rules, and one draw needn't show every extreme that they name: `live_rows`: each entry is a multiple of 256; some device has all 2048 rows live. Every block of lower_inv is lower triangular, and every block of upper_inv, sep_lower_inv and sep_upper_inv upper triangular, each with a diagonal between 1 and 1.5.
All inputs are finite; a program needn't handle non-finite values.
Results may differ from a plain program's by a relative error of at most 0.0055.
Values may be sent and summed in bfloat16 or wider, within the bound.
No kernel may reach another device: no remote copies, remote signals or barrier semaphores. Data moves between devices by JAX's collectives and lax.ppermute only.
A program may use at most 64 MiB of HBM per device.

v0:
```python
import jax
import jax.numpy as jnp
from jax import lax
from jax.sharding import PartitionSpec as P


def apply_blocks(vectors, inverse):
    vec_count = vectors.shape[0]
    shaped = vectors.astype(jnp.bfloat16).reshape(vec_count, inverse.shape[0], inverse.shape[1])
    product = jnp.einsum("vkr,krc->vkc", shaped, inverse, preferred_element_type=jnp.float32)
    return product.reshape(vec_count, inverse.shape[0] * inverse.shape[2])


def shards(
    rhs_sub,
    rhs_sep,
    live_rows,
    lower_inv,
    upper_inv,
    couple_low,
    couple_up,
    sep_lower_inv,
    sep_upper_inv,
    basis_sub,
    basis_sep,
):
    vec_count, row_count = rhs_sub.shape
    border = couple_low.shape[0]
    high = lax.Precision.HIGHEST
    live_mask = lax.broadcasted_iota(jnp.int32, (1, row_count), 1) < live_rows[0]
    lower_sol = jnp.where(live_mask, apply_blocks(rhs_sub, lower_inv), 0.0)
    border_rows = lower_sol[:, :border].astype(jnp.bfloat16)
    columns = couple_low
    top_block = lax.psum_scatter(
        lax.dot_general(
            columns, border_rows, (((0,), (1,)), ((), ())), preferred_element_type=jnp.float32
        ),
        "leaf",
        scatter_dimension=0,
        tiled=True,
    )
    top_block = lax.psum(top_block, "front")
    top_rhs = rhs_sep - top_block.T
    lower_part = jnp.dot(
        top_rhs.astype(jnp.bfloat16), sep_lower_inv, preferred_element_type=jnp.float32
    )
    top_lower = lax.psum(lower_part, "leaf")
    upper_part = lax.dot_general(
        top_lower.astype(jnp.bfloat16),
        sep_upper_inv,
        (((1,), (1,)), ((), ())),
        preferred_element_type=jnp.float32,
    )
    top_sol = lax.psum(upper_part, "front")
    columns = couple_up
    correction = lax.dot_general(
        lax.all_gather(top_sol.astype(jnp.bfloat16), "leaf", axis=1, tiled=True),
        columns,
        (((1,), (1,)), ((), ())),
        preferred_element_type=jnp.float32,
    )
    updated = jnp.concatenate([lower_sol[:, :border] - correction, lower_sol[:, border:]], axis=1)
    upper_sol = jnp.where(live_mask, apply_blocks(updated, upper_inv), 0.0)
    coef_sum = jnp.zeros((basis_sub.shape[0], vec_count), jnp.float32)
    for sweep in range(2):
        local_sub = lax.dot_general(basis_sub, upper_sol, (((1,), (1,)), ((), ())), precision=high)
        local_sep = lax.dot_general(basis_sep, top_sol, (((1,), (1,)), ((), ())), precision=high)
        coef_pass = lax.psum(local_sub, ("leaf", "front")) + lax.psum(local_sep, "leaf")
        part_sub = upper_sol
        part_sep = top_sol
        part_sub = part_sub - lax.dot_general(
            coef_pass, basis_sub, (((0,), (0,)), ((), ())), precision=high
        )
        part_sep = part_sep - lax.dot_general(
            coef_pass, basis_sep, (((0,), (0,)), ((), ())), precision=high
        )
        upper_sol = part_sub
        top_sol = part_sep
        coef_sum = coef_sum + coef_pass
    return (upper_sol, top_sol, coef_sum)


def solution(mesh):
    return jax.shard_map(
        shards,
        mesh=mesh,
        in_specs=(
            P(None, ("leaf", "front")),
            P(None, "leaf"),
            P(("leaf", "front")),
            P(("leaf", "front"), None, None),
            P(("leaf", "front"), None, None),
            P(("leaf", "front"), None),
            P(("leaf", "front"), None),
            P("leaf", "front"),
            P("leaf", "front"),
            P(None, ("leaf", "front")),
            P(None, "leaf"),
        ),
        out_specs=(P(None, ("leaf", "front")), P(None, "leaf"), P()),
        check_vma=False,
    )
```

profile of v0, /device:TPU:0, one launch (start us, length us, event | category | flops | bytes accessed | tf_op | source)
XLA Modules:
  0.0 882.8 jit_solution(9728875847282663332)
XLA Ops:
  7.2 0.0 copy-start
  7.2 0.0 reduce-scatter.2.cloned.1.call-start
  8.0 0.8 convert_element_type.20
  8.9 0.0 copy-start.6
  8.9 1.5 fusion.10
  10.4 0.0 copy-done
  10.4 0.0 copy-start.4
  10.4 1.2 convolution_bitcast_fusion
  11.6 0.0 reduce-scatter.2.cloned.1.call-update
  11.6 0.7 slice.16
  12.3 141.0 %reduce-scatter.2.cloned.1.call-done = f32[256,8]{0,1:T(8,128)} async-done(((f32[16384,8]{0,1:T(8,128)}), f32[256,8]{0,1:T(8,128)}) %reduce-scatter.2.cloned.1.call-update) | async-done | bytes 8208 | tf_op jit(solution)/shard_map/reduce_scatter | solution.py:34
  153.3 0.0 copy-done.4
  153.3 10.6 %psum.49 = f32[8,256]{1,0:T(8,128)S(1)} all-reduce(f32[8,256]{1,0:T(8,128)} %bitcast.49), channel_id=1, replica_groups=mesh['leaf'=64,'front'=4] {'front'}, use_global_device_ids=true, to_apply=%region_1.2 | all-reduce | flops 2048 | bytes 16384 | tf_op jit(solution)/shard_map/psum | solution.py:42
  163.9 0.0 copy-done.6
  163.9 2.0 fusion.6
  165.9 246.2 %all-reduce.1 = bf16[8,4096]{1,0:T(8,128)(2,1)S(1)} all-reduce(f32[8,4096]{1,0:T(8,128)S(1)} %fusion.6), channel_id=1, replica_groups=mesh['leaf'=64,'front'=4] {'leaf'}, use_global_device_ids=true, to_apply=%region_2.3 | all-reduce | flops 32768 | bytes 196608 | tf_op jit(solution)/shard_map/psum | solution.py:47
  412.0 0.0 copy-start.2
  412.0 2.9 fusion.12
  415.0 0.0 copy-start.1
  415.0 7.9 psum.51
  422.9 0.0 copy-start.5
  423.0 41.0 %all_gather.3 = bf16[8,16384]{1,0:T(8,128)(2,1)S(1)} all-gather(bf16[8,256]{1,0:T(8,128)(2,1)S(1)} %convert_element_type.24), channel_id=1, replica_groups=mesh['leaf'=64,'front'=4] {'leaf'}, dimensions={1}, use_global_device_ids=true | all-gather | bytes 266240 | tf_op jit(solution)/shard_map/all_gather | solution.py:57
  463.9 2.2 fusion
  466.2 0.0 copy-done.5
  466.2 0.1 pad_maximum_fusion
  466.3 0.0 copy-done.2
  466.3 0.2 fusion.11
  466.5 0.0 copy-start.3
  466.5 0.6 copy-done.3
  467.2 0.0 copy-done.1
  467.2 0.4 convolution_bitcast_fusion.4
  467.6 75.8 %psum.52 = f32[48,8]{0,1:T(8,128)S(1)} all-reduce(f32[48,8]{0,1:T(8,128)S(1)} %convolution_bitcast_fusion.4), channel_id=1, replica_groups=mesh['leaf'=64,'front'=4] {'leaf','front'}, use_global_device_ids=true, to_apply=%region_4.5 | all-reduce | flops 384 | bytes 3072 | tf_op jit(solution)/shard_map/psum | solution.py:68
  543.4 0.9 convolution_bitcast_fusion.2
  544.4 126.2 %psum.53 = f32[48,8]{0,1:T(8,128)S(1)} all-reduce(f32[48,8]{0,1:T(8,128)S(1)} %convolution_bitcast_fusion.2), channel_id=1, replica_groups=mesh['leaf'=64,'front'=4] {'leaf'}, use_global_device_ids=true, to_apply=%region_5.6 | all-reduce | flops 384 | bytes 3072 | tf_op jit(solution)/shard_map/psum | solution.py:68
  670.6 1.1 convolution_subtract_fusion.1
  671.7 0.9 convolution_subtract_fusion.3
  672.6 0.4 convolution_bitcast_fusion.3
  673.1 71.6 %psum.54 = f32[48,8]{0,1:T(8,128)S(1)} all-reduce(f32[48,8]{0,1:T(8,128)S(1)} %convolution_bitcast_fusion.3), channel_id=1, replica_groups=mesh['leaf'=64,'front'=4] {'leaf','front'}, use_global_device_ids=true, to_apply=%region_6.7 | all-reduce | flops 384 | bytes 3072 | tf_op jit(solution)/shard_map/psum | solution.py:68
  744.7 0.9 convolution_bitcast_fusion.1
  745.6 127.3 %psum.55 = f32[48,8]{0,1:T(8,128)S(1)} all-reduce(f32[48,8]{0,1:T(8,128)S(1)} %convolution_bitcast_fusion.1), channel_id=1, replica_groups=mesh['leaf'=64,'front'=4] {'leaf'}, use_global_device_ids=true, to_apply=%region_7.8 | all-reduce | flops 384 | bytes 3072 | tf_op jit(solution)/shard_map/psum | solution.py:68
  872.9 0.6 add_add_fusion
  873.5 1.5 convolution_subtract_fusion.2
  875.0 0.9 convolution_subtract_fusion
  (4 shorter events, 0.0 us)
Async XLA Ops:
  7.2 3.2 copy-start
  7.2 146.1 %reduce-scatter.2.cloned.1.call-start = ((), (), s32[]{:S(2)}) async-start(), calls=%async_computation.1 | async-start | bytes 532480 | tf_op jit(solution)/shard_map/reduce_scatter | solution.py:34
  8.9 155.0 %copy-start.6 = (f32[8,256]{1,0:T(8,128)S(1)}, f32[8,256]{1,0:T(8,128)}, u32[]{:S(2)}) copy-start(f32[8,256]{1,0:T(8,128)} %param.12) | copy-start | bytes 24580
  10.4 142.9 %copy-start.4 = (f32[8,2048]{1,0:T(8,128)}, f32[8,2048]{1,0:T(8,128)S(1)}, u32[]{:S(2)}) copy-start(f32[8,2048]{1,0:T(8,128)S(1)} %broadcast_select_fusion) | copy-start | bytes 196612
  412.0 54.2 %copy-start.2 = (bf16[8,256,256]{2,1,0:T(8,128)(2,1)S(1)}, bf16[8,256,256]{2,1,0:T(8,128)(2,1)}, u32[]{:S(2)}) copy-start(bf16[8,256,256]{2,1,0:T(8,128)(2,1)} %param.15) | copy-start | bytes 3145732
  415.0 52.2 %copy-start.1 = (f32[48,2048]{1,0:T(8,128)S(1)}, f32[48,2048]{1,0:T(8,128)}, u32[]{:S(2)}) copy-start(f32[48,2048]{1,0:T(8,128)} %param.20) | copy-start | bytes 1179652
  422.9 43.3 %copy-start.5 = (bf16[8,1984]{1,0:T(8,128)(2,1)S(1)}, bf16[8,1984]{1,0:T(8,128)(2,1)}, u32[]{:S(2)}) copy-start(bf16[8,1984]{1,0:T(8,128)(2,1)} %slice.16) | copy-start | bytes 95236
  466.5 0.6 copy-start.3
Sparse Core Ops, SparseCore 0:
  11.9 141.2 reduce-scatter.1
where the time goes:
time: 884 us; the launch traced here: 883 us
  blocking collectives  707 us (80%)
  waiting for transfers between devices  141 us (16%)
  matrix products  17.3 us (2%)
  between operations  14.9 us (2%)
    psum x2, blocking collectives, shards(): lax.psum(local_sep, 'leaf')  253 us
    psum x1, blocking collectives, shards(): top_lower = lax.psum(lower_part, 'leaf')  246 us
    psum x2, blocking collectives, shards(): lax.psum(local_sub, ('leaf', 'front')) + lax.psum(local_sep, 'leaf')  147 us
    reduce_scatter x1, waiting for transfers between devices, shards(): lax.psum_scatter(lax.dot_general(columns, border_rows, (((0,), (1,)), (()...  141 us
    all_gather x1, blocking collectives, shards(): lax.all_gather(top_sol.astype(jnp.bfloat16), 'leaf', axis=1, tiled=True)  41 us
  transfers between devices with their start and end apart: 1, of which 1 were waited for; matrix products, arithmetic and copies ran while one was open for 0% of the time, Pallas kernels for 0%

commit v1 on v0

--- a/solution.py
+++ b/solution.py
@@ -65,7 +65,7 @@
     for sweep in range(2):
         local_sub = lax.dot_general(basis_sub, upper_sol, (((1,), (1,)), ((), ())), precision=high)
         local_sep = lax.dot_general(basis_sep, top_sol, (((1,), (1,)), ((), ())), precision=high)
-        coef_pass = lax.psum(local_sub, ("leaf", "front")) + lax.psum(local_sep, "leaf")
+        coef_pass = lax.psum(lax.psum(local_sub, "front"), "leaf") + lax.psum(local_sep, "leaf")
         part_sub = upper_sol
         part_sep = top_sol
         part_sub = part_sub - lax.dot_general(

time: 884 us -> 752 us (0.85)
  blocking collectives: 707 us -> 572 us
    psum x4, blocking collectives: 401 us -> 267 us  [the longest x2 249 us: shards(): lax.psum(lax.psum(local_sub, 'front'), 'leaf') + lax.psum(local_sep, 'leaf')]
where the time goes in v1:
time: 752 us; the launch traced here: 748 us
  blocking collectives  572 us (76%)
  waiting for transfers between devices  141 us (19%)
  matrix products  17.3 us (2%)
  between operations  14.9 us (2%)
    psum x2, blocking collectives, shards(): lax.psum(lax.psum(local_sub, 'front'), 'leaf') + lax.psum(local_sep, 'leaf')  249 us
    psum x1, blocking collectives, shards(): top_lower = lax.psum(lower_part, 'leaf')  246 us
    reduce_scatter x1, waiting for transfers between devices, shards(): lax.psum_scatter(lax.dot_general(columns, border_rows, (((0,), (1,)), (()...  141 us
    all_gather x1, blocking collectives, shards(): lax.all_gather(top_sol.astype(jnp.bfloat16), 'leaf', axis=1, tiled=True)  41 us
    psum x2, blocking collectives, shards(): lax.psum(local_sub, 'front')  17.8 us
  transfers between devices with their start and end apart: 1, of which 1 were waited for; matrix products, arithmetic and copies ran while one was open for 0% of the time, Pallas kernels for 0%

profile of v1, /device:TPU:0, one launch (start us, length us, event | category | flops | bytes accessed | tf_op | source)
XLA Modules:
  0.0 748.5 jit_solution(13482672004256940074)
XLA Ops:
  7.2 0.0 copy-start
  7.2 0.0 reduce-scatter.2.cloned.1.call-start
  8.0 0.8 convert_element_type.20
  8.9 0.0 copy-start.6
  8.9 1.5 fusion.10
  10.4 0.0 copy-done
  10.4 0.0 copy-start.4
  10.4 1.2 convolution_bitcast_fusion
  11.6 0.0 reduce-scatter.2.cloned.1.call-update
  11.6 0.7 slice.16
  12.3 141.0 %reduce-scatter.2.cloned.1.call-done = f32[256,8]{0,1:T(8,128)} async-done(((f32[16384,8]{0,1:T(8,128)}), f32[256,8]{0,1:T(8,128)}) %reduce-scatter.2.cloned.1.call-update) | async-done | bytes 8208 | tf_op jit(solution)/shard_map/reduce_scatter | solution.py:34
  153.3 0.0 copy-done.4
  153.3 10.6 %psum.63 = f32[8,256]{1,0:T(8,128)S(1)} all-reduce(f32[8,256]{1,0:T(8,128)} %bitcast.55), channel_id=1, replica_groups=mesh['leaf'=64,'front'=4] {'front'}, use_global_device_ids=true, to_apply=%region_1.2 | all-reduce | flops 2048 | bytes 16384 | tf_op jit(solution)/shard_map/psum | solution.py:42
  163.9 0.0 copy-done.6
  163.9 2.0 fusion.8
  165.9 246.2 %all-reduce.1 = bf16[8,4096]{1,0:T(8,128)(2,1)S(1)} all-reduce(f32[8,4096]{1,0:T(8,128)S(1)} %fusion.8), channel_id=1, replica_groups=mesh['leaf'=64,'front'=4] {'leaf'}, use_global_device_ids=true, to_apply=%region_2.3 | all-reduce | flops 32768 | bytes 196608 | tf_op jit(solution)/shard_map/psum | solution.py:47
  412.0 0.0 copy-start.2
  412.0 2.9 fusion.12
  415.0 0.0 copy-start.1
  415.0 7.9 %psum.65 = f32[8,256]{1,0:T(8,128)S(1)} all-reduce(f32[8,256]{1,0:T(8,128)} %fusion.12), channel_id=1, replica_groups=mesh['leaf'=64,'front'=4] {'front'}, use_global_device_ids=true, to_apply=%region_3.4 | all-reduce | flops 2048 | bytes 16384 | tf_op jit(solution)/shard_map/psum | solution.py:54
  422.9 0.0 copy-start.5
  423.0 41.0 %all_gather.3 = bf16[8,16384]{1,0:T(8,128)(2,1)S(1)} all-gather(bf16[8,256]{1,0:T(8,128)(2,1)S(1)} %convert_element_type.24), channel_id=1, replica_groups=mesh['leaf'=64,'front'=4] {'leaf'}, dimensions={1}, use_global_device_ids=true | all-gather | bytes 266240 | tf_op jit(solution)/shard_map/all_gather | solution.py:57
  463.9 2.2 fusion.2
  466.2 0.0 copy-done.5
  466.2 0.1 pad_maximum_fusion
  466.3 0.0 copy-done.2
  466.3 0.2 fusion.11
  466.5 0.0 copy-start.3
  466.5 0.6 copy-done.3
  467.2 0.0 copy-done.1
  467.2 0.4 convolution_bitcast_fusion.4
  467.6 9.7 %psum.66 = f32[48,8]{0,1:T(8,128)S(1)} all-reduce(f32[48,8]{0,1:T(8,128)S(1)} %convolution_bitcast_fusion.4), channel_id=1, replica_groups=mesh['leaf'=64,'front'=4] {'front'}, use_global_device_ids=true, to_apply=%region_4.5 | all-reduce | flops 384 | bytes 3072 | tf_op jit(solution)/shard_map/psum | solution.py:68
  477.3 0.9 fusion.1
  478.2 124.8 %psum.72 = f32[48,8]{0,1:T(8,128)S(1)} all-reduce(f32[48,8]{0,1:T(8,128)S(1)} %fusion.1), channel_id=1, replica_groups=mesh['leaf'=64,'front'=4] {'leaf'}, use_global_device_ids=true, to_apply=%region_5.6 | all-reduce | flops 384 | bytes 3072 | tf_op jit(solution)/shard_map/psum | solution.py:68
  603.0 1.1 convolution_subtract_fusion.1
  604.2 0.9 convolution_subtract_fusion.3
  605.1 0.4 convolution_bitcast_fusion.3
  605.5 8.0 %psum.69 = f32[48,8]{0,1:T(8,128)S(1)} all-reduce(f32[48,8]{0,1:T(8,128)S(1)} %convolution_bitcast_fusion.3), channel_id=1, replica_groups=mesh['leaf'=64,'front'=4] {'front'}, use_global_device_ids=true, to_apply=%region_7.8 | all-reduce | flops 384 | bytes 3072 | tf_op jit(solution)/shard_map/psum | solution.py:68
  613.5 0.9 fusion
  614.5 124.1 %psum.73 = f32[48,8]{0,1:T(8,128)S(1)} all-reduce(f32[48,8]{0,1:T(8,128)S(1)} %fusion), channel_id=1, replica_groups=mesh['leaf'=64,'front'=4] {'leaf'}, use_global_device_ids=true, to_apply=%region_8.9 | all-reduce | flops 384 | bytes 3072 | tf_op jit(solution)/shard_map/psum | solution.py:68
  738.5 0.6 add.31
  739.1 1.5 convolution_subtract_fusion.2
  740.7 0.9 convolution_subtract_fusion
  (3 shorter events, 0.0 us)
Async XLA Ops:
  7.2 3.2 copy-start
  7.2 146.1 %reduce-scatter.2.cloned.1.call-start = ((), (), s32[]{:S(2)}) async-start(), calls=%async_computation.1 | async-start | bytes 532480 | tf_op jit(solution)/shard_map/reduce_scatter | solution.py:34
  8.9 155.0 %copy-start.6 = (f32[8,256]{1,0:T(8,128)S(1)}, f32[8,256]{1,0:T(8,128)}, u32[]{:S(2)}) copy-start(f32[8,256]{1,0:T(8,128)} %param.12) | copy-start | bytes 24580
  10.4 142.9 %copy-start.4 = (f32[8,2048]{1,0:T(8,128)}, f32[8,2048]{1,0:T(8,128)S(1)}, u32[]{:S(2)}) copy-start(f32[8,2048]{1,0:T(8,128)S(1)} %broadcast_select_fusion) | copy-start | bytes 196612
  412.0 54.2 %copy-start.2 = (bf16[8,256,256]{2,1,0:T(8,128)(2,1)S(1)}, bf16[8,256,256]{2,1,0:T(8,128)(2,1)}, u32[]{:S(2)}) copy-start(bf16[8,256,256]{2,1,0:T(8,128)(2,1)} %param.15) | copy-start | bytes 3145732
  415.0 52.2 %copy-start.1 = (f32[48,2048]{1,0:T(8,128)S(1)}, f32[48,2048]{1,0:T(8,128)}, u32[]{:S(2)}) copy-start(f32[48,2048]{1,0:T(8,128)} %param.20) | copy-start | bytes 1179652
  422.9 43.3 %copy-start.5 = (bf16[8,1984]{1,0:T(8,128)(2,1)S(1)}, bf16[8,1984]{1,0:T(8,128)(2,1)}, u32[]{:S(2)}) copy-start(bf16[8,1984]{1,0:T(8,128)(2,1)} %slice.16) | copy-start | bytes 95236
  466.5 0.6 copy-start.3
Sparse Core Ops, SparseCore 0:
  11.9 141.2 reduce-scatter.1
